TPU v7x, 512 devices: a whole 4x8x8 slice. The times are simulated.
512 devices in a mesh: seq: 32 (over z_lo, y, core), ch: 16 (over x, z_hi).
Axes of the slice: x: 4, y: 8, z: 8 (z_hi: 4, z_lo: 2; z = z_hi * 2 + z_lo), core: 2. Of those that a mesh axis runs over, the one named last changes fastest.
Arguments:
- tokens: bfloat16 [480, 65536], P('ch', 'seq'), may hold values from -6 to 6
- cotangent: bfloat16 [480, 65536], P('ch', 'seq'), may hold values from -6 to 6
- right_blocks: bfloat16 [16, 256, 256, 256], P('ch', 'seq'), may hold values from -0.375 to 0.375
- left_blocks: bfloat16 [16, 256, 256, 256], P('ch', 'seq'), may hold values from -0.375 to 0.375
- w_in: bfloat16 [480, 1920], P(None, 'ch'), may hold values from -0.25 to 0.25
- w_out: bfloat16 [1920, 480], P('ch'), may hold values from -0.125 to 0.125
Outputs:
- mixed: bfloat16 [480, 65536], P('ch', 'seq')
- grad_input: bfloat16 [480, 65536], P('ch', 'seq')
- grad_right: bfloat16 [16, 256, 256, 256], P('ch', 'seq')
- left_factor_gradient: bfloat16 [16, 256, 256, 256], P('ch', 'seq')
- grad_w_in: bfloat16 [480, 1920], P(None, 'ch')
- grad_w_out: bfloat16 [1920, 480], P('ch')
All inputs are finite; a program needn't handle non-finite values.
Results may differ from a plain program's by a relative error of at most 0.03.
Values may be sent and summed in bfloat16 or wider, within the bound.
A program may use at most 64 MiB of HBM per device.

v0:
```python
import jax
import jax.numpy as jnp
from jax import lax
from jax.sharding import PartitionSpec as P


def gelu_value(value_in):
    return 0.5 * value_in * (1.0 + lax.erf(value_in * 0.7071067811865476))


def gelu_slope(value_in):
    return (
        0.5 * (1.0 + lax.erf(value_in * 0.7071067811865476))
        + value_in * jnp.exp(-0.5 * value_in * value_in) * 0.3989422804014327
    )


def local(tokens, cotangent, right_blocks, left_blocks, w_in, w_out):
    group_ch = tokens.shape[0]
    positions = tokens.shape[1]
    right_local = right_blocks[0]
    left_factor_local = left_blocks[0]
    nblocks = right_local.shape[0]
    blk_width = right_local.shape[1]
    token_blocks = tokens.reshape(group_ch, nblocks, blk_width)
    block_layout = jnp.einsum(
        "ikj,cij->cki", right_local, token_blocks, preferred_element_type=jnp.float32
    ).astype(jnp.bfloat16)
    column_layout = lax.all_to_all(block_layout, "seq", split_axis=1, concat_axis=2, tiled=True)
    mixed_cols = jnp.einsum(
        "xns,oxs->onx", left_factor_local, column_layout, preferred_element_type=jnp.float32
    ).astype(jnp.bfloat16)
    column_layout, monarch_product = (
        column_layout,
        lax.all_to_all(mixed_cols, "seq", split_axis=1, concat_axis=2, tiled=True),
    )
    monarch_f = monarch_product.reshape(group_ch, positions).astype(jnp.float32)
    tokens_f = tokens.astype(jnp.float32)
    sigma = jax.nn.sigmoid(tokens_f)
    silu_x = tokens_f * sigma
    slope_silu = sigma * (1.0 + tokens_f * (1.0 - sigma))
    gate_out = (tokens_f + monarch_f * silu_x).astype(jnp.bfloat16)
    gate_full = lax.all_gather(gate_out, "ch", axis=0, tiled=True)
    pre_act = lax.dot_general(
        w_in, gate_full, (((0,), (0,)), ((), ())), preferred_element_type=jnp.float32
    )
    hidden = gelu_value(pre_act).astype(jnp.bfloat16)
    mlp_out = lax.psum_scatter(
        lax.dot_general(
            w_out, hidden, (((0,), (0,)), ((), ())), preferred_element_type=jnp.float32
        ).astype(jnp.bfloat16),
        "ch",
        scatter_dimension=0,
        tiled=True,
    ).astype(jnp.float32)
    mixed_out = (gate_out.astype(jnp.float32) + mlp_out).astype(jnp.bfloat16)
    cot_full = lax.all_gather(cotangent, "ch", axis=0, tiled=True)
    back_grad = jnp.dot(w_out, cot_full, preferred_element_type=jnp.float32)
    pre_grad = (back_grad * gelu_slope(pre_act)).astype(jnp.bfloat16)
    gate_grad = cotangent.astype(jnp.float32) + lax.psum_scatter(
        jnp.dot(w_in, pre_grad, preferred_element_type=jnp.float32).astype(jnp.bfloat16),
        "ch",
        scatter_dimension=0,
        tiled=True,
    ).astype(jnp.float32)
    monarch_product_gradient = (
        (gate_grad * silu_x).astype(jnp.bfloat16).reshape(group_ch, nblocks, blk_width)
    )
    column_gradient = lax.all_to_all(
        monarch_product_gradient, "seq", split_axis=2, concat_axis=1, tiled=True
    )
    left_factor_gradient = jnp.einsum(
        "pux,pxd->xud", column_gradient, column_layout, preferred_element_type=jnp.float32
    ).astype(jnp.bfloat16)
    mixed_grad = jnp.einsum(
        "gwa,qwg->qga", left_factor_local, column_gradient, preferred_element_type=jnp.float32
    ).astype(jnp.bfloat16)
    block_layout_gradient = lax.all_to_all(
        mixed_grad, "seq", split_axis=2, concat_axis=1, tiled=True
    )
    grad_right = jnp.einsum(
        "cki,cij->ikj", block_layout_gradient, token_blocks, preferred_element_type=jnp.float32
    ).astype(jnp.bfloat16)
    from_right = jnp.einsum(
        "ikj,cki->cij", right_local, block_layout_gradient, preferred_element_type=jnp.float32
    ).reshape(group_ch, positions)
    grad_input = (gate_grad * (1.0 + monarch_f * slope_silu) + from_right).astype(jnp.bfloat16)
    term_in = lax.dot_general(
        gate_full, pre_grad, (((1,), (1,)), ((), ())), preferred_element_type=jnp.float32
    )
    term_out = lax.dot_general(
        cot_full, hidden, (((1,), (1,)), ((), ())), preferred_element_type=jnp.float32
    )
    stacked = jnp.stack([term_in, term_out])
    summed = lax.psum(stacked.astype(jnp.bfloat16), "seq")
    grad_w_in = summed[0]
    grad_w_out = summed[1].T
    return (
        mixed_out,
        grad_input,
        grad_right[None],
        left_factor_gradient[None],
        grad_w_in,
        grad_w_out,
    )


def solution(mesh):
    placed = (
        P("ch", "seq"),
        P("ch", "seq"),
        P("ch", "seq", None, None),
        P("ch", "seq", None, None),
        P(None, "ch"),
        P("ch", None),
    )
    return jax.shard_map(
        local,
        mesh=mesh,
        in_specs=placed,
        out_specs=(
            P("ch", "seq"),
            P("ch", "seq"),
            P("ch", "seq", None, None),
            P("ch", "seq", None, None),
            P(None, "ch"),
            P("ch", None),
        ),
        check_vma=False,
    )
```

profile of v0, /device:TPU:1, one launch (start us, length us, event | category | flops | bytes accessed | tf_op | source)
XLA Modules:
  0.0 502.0 jit_solution(9354347490571395537)
XLA Ops:
  7.2 0.7 all-gather.7.cloned.1.call-update
  8.0 0.9 copy.126
  8.9 0.6 copy-done.9
  9.6 1.6 fusion.7
  11.2 0.4 copy.99
  11.6 0.9 reshape.38
  12.5 19.4 %all_to_all.63 = bf16[32,2,960]{2,1,0:T(2,128)(2,1)S(1)} all-to-all(bf16[32,2,960]{2,1,0:T(2,128)(2,1)S(1)} %reshape.38), channel_id=1, replica_groups=mesh['seq'=32,'ch'=16] {'seq'}, dimensions={0} | all-to-all | bytes 245760 | tf_op jit(solution)/shard_map/all_to_all | solution.py:29
  31.9 1.4 reshape.39
  33.3 0.4 fusion.9
  33.7 0.4 copy.102
  34.1 0.9 reshape.40
  35.0 13.4 %all_to_all.64 = bf16[32,2,960]{2,1,0:T(2,128)(2,1)S(1)} all-to-all(bf16[32,2,960]{2,1,0:T(2,128)(2,1)S(1)} %reshape.40), channel_id=1, replica_groups=mesh['seq'=32,'ch'=16] {'seq'}, dimensions={0} | all-to-all | bytes 245760 | tf_op jit(solution)/shard_map/all_to_all | solution.py:35
  48.4 1.4 reshape.41
  50.3 0.5 copy-done.7
  50.8 0.8 fusion.27
  51.7 1.3 dynamic-slice.6
  53.6 27.8 %all-gather.7.cloned.1.call-done = bf16[16,30,2048]{2,1,0:T(8,128)(2,1)} async-done(((bf16[1,30,2048]{2,1,0:T(8,128)(2,1)}), bf16[16,30,2048]{2,1,0:T(8,128)(2,1)}) %all-gather.7.cloned.1.call-update) | async-done | bytes 1966096 | tf_op jit(solution)/shard_map/all_gather | solution.py:57
  81.4 2.8 reshape.35
  84.2 64.1 %all-gather.5.cloned.1.call-done = bf16[16,30,2048]{2,1,0:T(8,128)(2,1)} async-done(((bf16[1,30,2048]{2,1,0:T(8,128)(2,1)}), bf16[16,30,2048]{2,1,0:T(8,128)(2,1)}) %all-gather.5.cloned.1.call-update) | async-done | bytes 1966096 | tf_op jit(solution)/shard_map/all_gather | solution.py:43
  148.3 1.8 reshape.33
  150.2 1.6 multiply_convert_fusion
  151.8 0.7 fusion.4
  152.6 1.3 fusion.10
  153.9 1.9 fusion.3
  155.8 2.0 fusion.2
  157.9 98.8 %fusion.37 = (bf16[32,2048]{1,0:T(8,128)(2,1)}, bf16[32,2048]{1,0:T(8,128)(2,1)}) fusion(bf16[480,2048]{1,0:T(8,128)(2,1)} %fusion.2, bf16[480,2048]{1,0:T(8,128)(2,1)} %fusion.3), kind=kCustom, calls=%all-reduce-scatter.2 | all-reduce-scatter fusion | flops 2097153 | bytes 4196352
  256.7 1.6 slice.11
  258.3 1.9 collective-permute-start.1
  260.3 1.7 fusion.11
  262.0 0.7 pad_maximum_fusion
  262.8 1.0 slice.10
  263.8 1.5 collective-permute-start
  265.2 2.0 concatenate.1
  267.3 1.1 multiply_convert_fusion.1
  268.8 1.6 reshape.42
  270.3 14.2 %all-to-all-start.2 = ((bf16[32,2,960]{2,1,0:T(2,128)(2,1)}), bf16[32,2,960]{2,1,0:T(2,128)(2,1)S(1)}, u32[]{:S(2)}, u32[]{:S(2)}) async-start(bf16[32,2,960]{2,1,0:T(2,128)(2,1)} %reshape.42), calls=%async_computation.2 | async-start | bytes 262144 | tf_op jit(solution)/shard_map/all_to_all | solution.py:69
  284.9 0.7 add_convert_fusion
  285.6 8.1 %all-to-all-done.2 = bf16[32,2,960]{2,1,0:T(2,128)(2,1)S(1)} async-done(((bf16[32,2,960]{2,1,0:T(2,128)(2,1)}), bf16[32,2,960]{2,1,0:T(2,128)(2,1)S(1)}, u32[]{:S(2)}, u32[]{:S(2)}) %all-to-all-start.2) | async-done | bytes 122912 | tf_op jit(solution)/shard_map/all_to_all | solution.py:69
  293.7 1.4 reshape.43
  296.2 1.6 reshape.44
  297.7 5.1 %all-to-all-start.3 = ((bf16[32,2,960]{2,1,0:T(2,128)(2,1)}), bf16[32,2,960]{2,1,0:T(2,128)(2,1)S(1)}, u32[]{:S(2)}, u32[]{:S(2)}) async-start(bf16[32,2,960]{2,1,0:T(2,128)(2,1)} %reshape.44), calls=%async_computation.3 | async-start | bytes 262144 | tf_op jit(solution)/shard_map/all_to_all | solution.py:78
  302.8 184.0 %all-reduce.7.cloned.1.call-done = bf16[2,480,120]{2,1,0:T(8,128)(2,1)} async-done(((bf16[2,480,120]{2,1,0:T(8,128)(2,1)}), bf16[2,480,120]{2,1,0:T(8,128)(2,1)}) %all-reduce.7.cloned.1.call-update) | async-done | bytes 230416 | tf_op jit(solution)/shard_map/psum | solution.py:95
  486.9 1.6 slice_bitcast_fusion
  488.5 0.8 copy.120
  489.2 1.5 fusion.6
  490.7 1.4 reshape.45
  492.9 1.5 fusion.5
  494.7 0.8 fusion.34
  (58 shorter events, 3.5 us)
Async XLA Ops:
  7.2 26.1 %copy-start = (bf16[1,8,256,256]{3,2,1,0:T(8,128)(2,1)S(1)}, bf16[1,8,256,256]{3,2,1,0:T(8,128)(2,1)}, u32[]{:S(2)}) copy-start(bf16[1,8,256,256]{3,2,1,0:T(8,128)(2,1)} %param.9) | copy-start | bytes 3145732
  7.2 74.2 %all-gather.7.cloned.1.call-start = ((), (), s32[]{:S(2)}) async-start(), calls=%async_computation.6 | async-start | bytes 2228224 | tf_op jit(solution)/shard_map/all_gather | solution.py:57
  7.9 140.4 %all-gather.5.cloned.1.call-start = ((), (), s32[]{:S(2)}) async-start(), calls=%async_computation.5 | async-start | bytes 2228224 | tf_op jit(solution)/shard_map/all_gather | solution.py:43
  8.9 0.7 copy-start.9
  49.9 0.9 copy-start.7
  50.8 33.4 %copy-start.5 = (f32[30,2048]{1,0:T(8,128)}, f32[30,2048]{1,0:T(8,128)S(1)}, u32[]{:S(2)}) copy-start(f32[30,2048]{1,0:T(8,128)S(1)} %copy.104) | copy-start | bytes 737284
  51.6 435.2 %all-reduce.7.cloned.1.call-start = ((), (), s32[]{:S(2)}) async-start(), calls=%async_computation.4 | async-start | bytes 491520 | tf_op jit(solution)/shard_map/psum | solution.py:95
  150.2 1.6 copy-start.1
  150.2 1.6 copy-start.16
  151.8 4.1 copy-start.3
  152.5 1.4 copy-start.14
  157.8 102.4 %copy-start.2 = (bf16[480,2048]{1,0:T(8,128)(2,1)S(1)}, bf16[480,2048]{1,0:T(8,128)(2,1)}, u32[]{:S(2)}) copy-start(bf16[480,2048]{1,0:T(8,128)(2,1)} %reshape.35) | copy-start | bytes 5898244
  256.7 5.3 %copy-start.15 = (bf16[1,480,120]{2,1,0:T(8,128)(2,1)S(1)}, bf16[1,480,120]{2,1,0:T(8,128)(2,1)}, u32[]{:S(2)}) copy-start(bf16[1,480,120]{2,1,0:T(8,128)(2,1)} %fusion.10) | copy-start | bytes 345604
  258.3 6.9 %collective-permute-start.1 = (bf16[30,2048]{1,0:T(8,128)(2,1)}, bf16[30,2048]{1,0:T(8,128)(2,1)}, u32[]{:S(2)}, u32[]{:S(2)}) collective-permute-start(bf16[30,2048]{1,0:T(8,128)(2,1)} %slice.11), channel_id=1, source_target_pairs={{0,1},{1,2},{2,3},{3,4},{4,5},{5,6},{6,7},{7,8},{8,9},{9,10},{10,1... | collective-permute-start | bytes 368648
  262.0 22.6 %copy-start.12 = (bf16[32,2048]{1,0:T(8,128)(2,1)S(1)}, bf16[32,2048]{1,0:T(8,128)(2,1)}, u32[]{:S(2)}) copy-start(bf16[32,2048]{1,0:T(8,128)(2,1)} %get-tuple-element.38) | copy-start | bytes 393220
  262.8 22.1 %copy-start.11 = (bf16[30,2048]{1,0:T(8,128)(2,1)S(1)}, bf16[30,2048]{1,0:T(8,128)(2,1)}, u32[]{:S(2)}) copy-start(bf16[30,2048]{1,0:T(8,128)(2,1)} %fusion.27) | copy-start | bytes 368644
  263.8 20.8 %collective-permute-start = (bf16[30,2048]{1,0:T(8,128)(2,1)S(1)}, bf16[30,2048]{1,0:T(8,128)(2,1)S(1)}, u32[]{:S(2)}, u32[]{:S(2)}) collective-permute-start(bf16[30,2048]{1,0:T(8,128)(2,1)S(1)} %slice.10), channel_id=1, source_target_pairs={{0,1},{1,2},{2,3},{3,4},{4,5},{5,6},{6,7},{7,8},{8,9},{9,10},{10,1... | collective-permute-start | bytes 368648
  270.3 23.3 %all-to-all-start.2 = ((bf16[32,2,960]{2,1,0:T(2,128)(2,1)}), bf16[32,2,960]{2,1,0:T(2,128)(2,1)S(1)}, u32[]{:S(2)}, u32[]{:S(2)}) async-start(bf16[32,2,960]{2,1,0:T(2,128)(2,1)} %reshape.42), calls=%async_computation.2 | async-start | bytes 262144 | tf_op jit(solution)/shard_map/all_to_all | solution.py:69
  297.7 193.0 %all-to-all-start.3 = ((bf16[32,2,960]{2,1,0:T(2,128)(2,1)}), bf16[32,2,960]{2,1,0:T(2,128)(2,1)S(1)}, u32[]{:S(2)}, u32[]{:S(2)}) async-start(bf16[32,2,960]{2,1,0:T(2,128)(2,1)} %reshape.44), calls=%async_computation.3 | async-start | bytes 262144 | tf_op jit(solution)/shard_map/all_to_all | solution.py:78
  489.2 3.3 copy-start.4
  490.7 2.2 copy-start.10
  492.6 2.1 copy-start.6
  492.6 2.1 copy-start.8
  492.6 2.1 copy-start.13
Sparse Core Ops, SparseCore 0:
  11.0 70.3 all-gather.6
  85.0 63.2 all-gather.4
  262.9 223.9 all-reduce.6
where the time goes:
time: 503 us; the launch traced here: 502 us
  waiting for transfers between devices  285 us (57%)
  blocking collectives  132 us (26%)
  local copies, waits for them, and re-layouts  28.9 us (6%)
  starting transfers between devices  22.8 us (5%)
  matrix products  14.8 us (3%)
  between operations  14.8 us (3%)
    psum x1, waiting for transfers between devices, local(): summed = lax.psum(stacked.astype(jnp.bfloat16), 'seq')  184 us
    unnamed x1, blocking collectives  98.8 us
    all_gather x1, waiting for transfers between devices, local(): gate_full = lax.all_gather(gate_out, 'ch', axis=0, tiled=True)  64.1 us
    all_gather x1, waiting for transfers between devices, local(): cot_full = lax.all_gather(cotangent, 'ch', axis=0, tiled=True)  27.8 us
    unnamed x54, local copies, waits for them, and re-layouts  24.3 us
    all_to_all x1, blocking collectives, local(): lax.all_to_all(block_layout, 'seq', split_axis=1, concat_axis=2, tiled=True)  19.4 us
    all_to_all x1, starting transfers between devices, local(): lax.all_to_all(monarch_product_gradient, 'seq', split_axis=2, concat_axis...  14.2 us
    all_to_all x1, blocking collectives, local(): lax.all_to_all(mixed_cols, 'seq', split_axis=1, concat_axis=2, tiled=True)  13.4 us
  transfers between devices with their start and end apart: 7, of which 4 were waited for; matrix products, arithmetic and copies ran while one was open for 6% of the time, Pallas kernels for 0%

commit v1 on v0

v1 whole, which is shorter than its diff:
```python
import jax
import jax.numpy as jnp
from jax import lax
from jax.experimental import pallas as pl
from jax.experimental.pallas import tpu as pltpu
from jax.sharding import PartitionSpec as P

NS = 32
NC = 16
GC = 30
HID = 120
F32 = jnp.float32
BF16 = jnp.bfloat16
MESH = pl.DeviceIdType.MESH

NN = (((1,), (0,)), ((), ()))
NT = (((1,), (1,)), ((), ()))
TN = (((0,), (0,)), ((), ()))

A1, A2, A3, A4, XC, WT, XG, XU, XM, GX, GS, GA = range(12)


def dot(a, b, dims=NN):
    return lax.dot_general(a, b, dims, preferred_element_type=F32)


def one_hot(shape, test):
    rows = lax.broadcasted_iota(jnp.int32, shape, 0)
    cols = lax.broadcasted_iota(jnp.int32, shape, 1)
    return jnp.where(test(rows, cols), 1.0, 0.0).astype(BF16)


def gelu_parts(v):
    cdf = 0.5 * (1.0 + lax.erf(v * 0.7071067811865476))
    return v * cdf, cdf + v * jnp.exp(-0.5 * v * v) * 0.3989422804014327


def kernel(
    tok_h, cot_h, r_h, l_h, wi_h, wo_h,
    mixed_h, gin_h, gr_h, gl_h, gwi_h, gwo_h,
    tok_v, cot_v, r_v, l_v, wi_v, wo_v,
    tokp, cots, s1, r1, s2, r2, s3, r3, s4, r4,
    fold_src, ct, mon, go, gf, cf, ws, w12, w1t, w2t, back, hid, pg,
    su, ru, sm, rm, sg, rg, sh, rh, sf, rf, gg,
    mixed_v, gin_v, gl_v, gr_v, gwi_v, gwo_v,
    in_sem, out_sem, send_sem, recv_sem,
):
    s, c = lax.axis_index("seq"), lax.axis_index("ch")
    cx, cz = c // 4, lax.rem(c, 4)

    barrier = pltpu.get_barrier_semaphore()

    @pl.loop(1, NS)
    def _(o):
        pl.semaphore_signal(barrier, inc=1, device_id={"seq": lax.rem(s + o, NS), "ch": c}, device_id_type=MESH)

    @pl.loop(1, NC)
    def _(o):
        pl.semaphore_signal(barrier, inc=1, device_id={"seq": s, "ch": lax.rem(c + o, NC)}, device_id_type=MESH)

    ins = [
        pltpu.make_async_copy(src, dst, in_sem.at[n])
        for n, (src, dst) in enumerate(
            ((tok_h, tok_v), (r_h, r_v), (cot_h, cot_v), (wi_h, wi_v), (wo_h, wo_v), (l_h, l_v))
        )
    ]
    for copy in ins:
        copy.start()

    def send(which, src, dst, seq, ch):
        pltpu.make_async_remote_copy(
            src_ref=src, dst_ref=dst, send_sem=send_sem.at[which], recv_sem=recv_sem.at[which],
            device_id={"seq": seq, "ch": ch}, device_id_type=MESH,
        ).start()

    def over_seq(which, src_of, dst):
        @pl.loop(1, NS)
        def _(o):
            t = lax.rem(s + o, NS)
            send(which, src_of(t), dst.at[s], t, c)

    def arrived(which, view):
        pltpu.make_async_copy(view, view, recv_sem.at[which]).wait()

    def sent(which, view):
        pltpu.make_async_copy(view, view, send_sem.at[which]).wait()

    eye = one_hot((256, 256), lambda a, b: a == b)
    fold_t = one_hot((32, 256), lambda a, b: a == (b & 31))
    keep = (
        (lax.broadcasted_iota(jnp.int32, (8, 256), 1) >> 5) == lax.broadcasted_iota(jnp.int32, (8, 256), 0)
    )[None]

    def spread(n):
        row = jnp.broadcast_to(fold_src[:, n : n + 1, :], (NS, 8, 256))
        return jnp.where(keep, row, 0.0).reshape(256, 256).astype(BF16)

    def flip(rows, dst):
        stacked = jnp.concatenate([row.astype(BF16) for row in rows], axis=0)
        dst[...] = dot(eye, stacked, NT).reshape(NS, 8, 256).astype(BF16)

    ins[0].wait()
    tokp[...] = jnp.zeros_like(tokp)
    for i in range(8):
        tokp[i, 0:GC, :] = tok_v[:, 256 * i : 256 * i + 256]
    ins[1].wait()
    flip([dot(tokp[i], r_v[i], NT) for i in range(8)], s1)
    r1[s] = s1[s]

    ins[2].wait()
    cots[...] = jnp.zeros_like(cots)
    for q in range(4):
        cots[q, 0:GC, :] = cot_v[:, 512 * q : 512 * q + 512]
    cf[c] = cots[cx]
    pad_cols = one_hot(
        (GC * NC, 512), lambda a, b: (a == GC * (b >> 5) + (b & 31)) & ((b & 31) < GC)
    )
    ins[3].wait()
    ins[4].wait()
    ws[...] = jnp.zeros_like(ws)
    ws[0, 0:HID, :] = dot(wi_v[...], pad_cols, TN).astype(BF16)
    ws[1, 0:HID, :] = dot(wo_v[...], pad_cols).astype(BF16)
    w12[cx] = ws[...]

    pl.semaphore_wait(barrier, NS + NC - 2)
    over_seq(A1, lambda t: s1.at[t], r1)

    @pl.loop(1, NC)
    def _(o):
        t = lax.rem(c + o, NC)
        send(XC, cots.at[t // 4], cf.at[c], s, t)

    @pl.loop(1, 4)
    def _(o):
        t = lax.rem(cx + o, 4) * 4 + cz
        send(WT, ws, w12.at[cx], s, t)

    ins[5].wait()
    arrived(A1, r1.at[pl.ds(0, NS - 1)])
    fold_src[...] = r1[...].astype(F32)
    for k in range(8):
        ct[k] = dot(fold_t, spread(k), NT).astype(BF16)
    flip([dot(ct[k], l_v[k], NT) for k in range(8)], s2)
    r2[s] = s2[s]
    over_seq(A2, lambda t: s2.at[t], r2)

    arrived(WT, w12.at[pl.ds(0, 3)])
    eye128 = one_hot((128, 128), lambda a, b: a == b)
    for b in range(4):
        for h in range(4):
            cols = slice(128 * b, 128 * b + 128)
            w1t[b, :, 128 * h : 128 * h + 128] = dot(eye128, w12[h, 0, :, cols], NT).astype(BF16)
            w2t[b, :, 128 * h : 128 * h + 128] = dot(eye128, w12[h, 1, :, cols], NT).astype(BF16)
    arrived(XC, cf.at[pl.ds(0, NC - 1)])
    cot_all = cf[...].reshape(512, 512)
    for h in range(4):
        back[h] = dot(w12[h, 1], cot_all)

    arrived(A2, r2.at[pl.ds(0, NS - 1)])
    fold_src[...] = r2[...].astype(F32)
    for l in range(8):
        m = dot(fold_t, spread(l), NT)
        mon[l] = m
        t = tokp[l].astype(F32)
        go[l // 2, :, 256 * (l % 2) : 256 * (l % 2) + 256] = (t + m * (t * jax.nn.sigmoid(t))).astype(BF16)
    gf[c] = go[cx]

    @pl.loop(1, NC)
    def _(o):
        t = lax.rem(c + o, NC)
        send(XG, go.at[t // 4], gf.at[c], s, t)

    arrived(XG, gf.at[pl.ds(0, NC - 1)])
    gate_all = gf[...].reshape(512, 512)
    for h in range(4):
        value, slope = gelu_parts(dot(w12[h, 0], gate_all))
        hid[h] = value.astype(BF16)
        pg[h] = (back[h] * slope).astype(BF16)

    def partials(which, weights, units, dst, remote):
        all_units = units[...].reshape(512, 512)
        for j in range(4):
            b = lax.rem(cx + j, 4)
            dst[pl.ds(4 * b, 4)] = dot(weights[b], all_units).reshape(4, 32, 512).astype(BF16)
            for m in range(4):
                t = 4 * b + lax.rem(cz + m, 4)
                if j == 0 and m == 0:
                    continue
                send(which, dst.at[t], remote.at[c], s, t)
        remote[c] = dst[c]

    partials(XU, w1t, pg, su, ru)

    for h in range(4):
        sg[h, 0] = dot(pg[h], gate_all, NT).astype(BF16)
        sg[h, 1] = dot(hid[h], cot_all, NT).astype(BF16)
    rg[cx] = sg[cx]

    @pl.loop(1, 4)
    def _(o):
        x = lax.rem(cx + o, 4)
        send(GX, sg.at[x], rg.at[cx], s, x * 4 + cz)

    partials(XM, w2t, hid, sm, rm)

    arrived(XU, ru.at[pl.ds(0, NC - 1)])

    def summed(parts, l):
        q, at = l // 2, slice(256 * (l % 2), 256 * (l % 2) + 256)
        total = parts[4 * q, :, at].astype(F32)
        for z in range(1, 4):
            total = total + parts[4 * q + z, :, at].astype(F32)
        return total

    rows = []
    for l in range(8):
        t = tokp[l].astype(F32)
        g = cots[l // 2, :, 256 * (l % 2) : 256 * (l % 2) + 256].astype(F32) + summed(ru, l)
        gg[l] = g
        rows.append(g * (t * jax.nn.sigmoid(t)))
    flip(rows, s3)
    r3[s] = s3[s]
    over_seq(A3, lambda t: s3.at[t], r3)

    arrived(GX, rg.at[pl.ds(0, 3)])
    for n in range(2):
        total = rg[0, n].astype(F32)
        for x in range(1, 4):
            total = total + rg[x, n].astype(F32)
        sh[16 * n : 16 * n + 16] = total.reshape(16, 8, 512).astype(BF16)
    rh[s] = sh[s]
    over_seq(GS, lambda t: sh.at[t], rh)

    arrived(A3, r3.at[pl.ds(0, NS - 1)])
    fold_src[...] = r3[...].astype(F32)
    flip([dot(dot(fold_t, spread(k), NT).astype(BF16), l_v[k]) for k in range(8)], s4)
    r4[s] = s4[s]
    over_seq(A4, lambda t: s4.at[t], r4)

    arrived(GS, rh.at[pl.ds(0, NS - 1)])
    sf[...] = jnp.sum(rh[...].astype(F32), axis=0).astype(BF16)
    rf[s] = sf[...]
    over_seq(GA, lambda t: sf, rf)

    for k in range(8):
        g = dot(spread(k), fold_t, NT).astype(BF16)
        gl_v[k] = dot(g, ct[k]).astype(BF16)

    arrived(XM, rm.at[pl.ds(0, NC - 1)])
    for l in range(8):
        at = slice(256 * (l % 2), 256 * (l % 2) + 256)
        value = (go[l // 2, :, at].astype(F32) + summed(rm, l)).astype(BF16)
        mixed_v[:, 256 * l : 256 * l + 256] = value[0:GC]
    outs = [pltpu.make_async_copy(gl_v, gl_h, out_sem.at[0]), pltpu.make_async_copy(mixed_v, mixed_h, out_sem.at[1])]
    for copy in outs:
        copy.start()

    arrived(A4, r4.at[pl.ds(0, NS - 1)])
    fold_src[...] = r4[...].astype(F32)
    for i in range(8):
        x = spread(i)
        g = dot(x, fold_t, NT).astype(BF16)
        g_t = dot(fold_t, x, NT).astype(BF16)
        gr_v[i] = dot(g, tokp[i]).astype(BF16)
        t = tokp[i].astype(F32)
        sigma = jax.nn.sigmoid(t)
        through = gg[i] * (1.0 + mon[i] * (sigma * (1.0 + t * (1.0 - sigma))))
        value = (through + dot(g_t, r_v[i])).astype(BF16)
        gin_v[:, 256 * i : 256 * i + 256] = value[0:GC]
    outs += [pltpu.make_async_copy(gr_v, gr_h, out_sem.at[2]), pltpu.make_async_copy(gin_v, gin_h, out_sem.at[3])]
    for copy in outs[2:]:
        copy.start()

    arrived(GA, rf.at[pl.ds(0, NS - 1)])
    gwi_v[...] = dot(pad_cols, rf[0:16].reshape(128, 512), NT)[:, 0:HID].astype(BF16)
    gwo_v[...] = dot(rf[16:32].reshape(128, 512), pad_cols, NT)[0:HID].astype(BF16)
    outs += [pltpu.make_async_copy(gwi_v, gwi_h, out_sem.at[4]), pltpu.make_async_copy(gwo_v, gwo_h, out_sem.at[5])]
    for copy in outs[4:]:
        copy.start()

    for which, view in (
        (A1, s1.at[pl.ds(0, NS - 1)]), (A2, s2.at[pl.ds(0, NS - 1)]), (A3, s3.at[pl.ds(0, NS - 1)]),
        (A4, s4.at[pl.ds(0, NS - 1)]), (XC, cf.at[pl.ds(0, NC - 1)]), (WT, w12.at[pl.ds(0, 3)]),
        (XG, gf.at[pl.ds(0, NC - 1)]), (XU, su.at[pl.ds(0, NC - 1)]),
        (XM, sm.at[pl.ds(0, NC - 1)]), (GX, sg.at[pl.ds(0, 3)]), (GS, sh.at[pl.ds(0, NS - 1)]),
        (GA, rf.at[pl.ds(0, NS - 1)]),
    ):
        sent(which, view)
    for copy in outs:
        copy.wait()


def local(tokens, cotangent, right_blocks, left_blocks, w_in, w_out):
    piece = (NS, 8, 256)
    scratch = [
        ((GC, 2048), BF16), ((GC, 2048), BF16), ((8, 256, 256), BF16), ((8, 256, 256), BF16),
        ((480, HID), BF16), ((HID, 480), BF16),
        ((8, 32, 256), BF16), ((4, 32, 512), BF16),
        (piece, BF16), (piece, BF16), (piece, BF16), (piece, BF16),
        (piece, BF16), (piece, BF16), (piece, BF16), (piece, BF16),
        (piece, F32), ((8, 32, 256), BF16), ((8, 32, 256), F32),
        ((4, 32, 512), BF16), ((16, 32, 512), BF16), ((16, 32, 512), BF16),
        ((2, 128, 512), BF16), ((4, 2, 128, 512), BF16),
        ((4, 128, 512), BF16), ((4, 128, 512), BF16), ((4, 128, 512), F32),
        ((4, 128, 512), BF16), ((4, 128, 512), BF16),
        ((16, 32, 512), BF16), ((16, 32, 512), BF16), ((16, 32, 512), BF16), ((16, 32, 512), BF16),
        ((4, 2, 128, 512), BF16), ((4, 2, 128, 512), BF16),
        ((NS, 8, 512), BF16), ((NS, 8, 512), BF16), ((8, 512), BF16), ((NS, 8, 512), BF16),
        ((8, 32, 256), F32),
        ((GC, 2048), BF16), ((GC, 2048), BF16), ((8, 256, 256), BF16), ((8, 256, 256), BF16),
        ((480, HID), BF16), ((HID, 480), BF16),
    ]
    shapes = [
        ((GC, 2048), BF16), ((GC, 2048), BF16), ((8, 256, 256), BF16), ((8, 256, 256), BF16),
        ((480, HID), BF16), ((HID, 480), BF16),
    ]
    mixed, gin, gr, gl, gwi, gwo = pl.pallas_call(
        kernel,
        out_shape=[jax.ShapeDtypeStruct(*shape) for shape in shapes],
        in_specs=[pl.BlockSpec(memory_space=pl.ANY)] * 6,
        out_specs=[pl.BlockSpec(memory_space=pl.ANY)] * 6,
        scratch_shapes=[pltpu.VMEM(*shape) for shape in scratch]
        + [pltpu.SemaphoreType.DMA((6,)), pltpu.SemaphoreType.DMA((6,))]
        + [pltpu.SemaphoreType.DMA((12,)), pltpu.SemaphoreType.DMA((12,))],
        compiler_params=pltpu.CompilerParams(
            collective_id=0, has_side_effects=True, vmem_limit_bytes=48 * 1024 * 1024
        ),
        name="monarch_block",
    )(tokens, cotangent, right_blocks[0], left_blocks[0], w_in, w_out)
    return mixed, gin, gr[None], gl[None], gwi, gwo


def solution(mesh):
    placed = (
        P("ch", "seq"),
        P("ch", "seq"),
        P("ch", "seq", None, None),
        P("ch", "seq", None, None),
        P(None, "ch"),
        P("ch", None),
    )
    return jax.shard_map(
        local,
        mesh=mesh,
        in_specs=placed,
        out_specs=placed,
        check_vma=False,
    )
```

time: 503 us -> 106 us (0.21)
  waiting for transfers between devices: 285 us -> 0 us
  blocking collectives: 132 us -> 0 us
  Pallas kernels: 0 us -> 94.4 us
  starting transfers between devices: 22.8 us -> 0 us
  local copies, waits for them, and re-layouts: 28.9 us -> 10.6 us
  matrix products: 14.8 us -> 0 us
  between operations: 14.8 us -> 0.66 us
    psum x1 -> x0, waiting for transfers between devices: 184 us -> none  [local(): summed = lax.psum(stacked.astype(jnp.bfloat16), 'seq')]
    unnamed x1 -> x0, blocking collectives: 98.8 us -> none
    pallas_call x0 -> x1, Pallas kernels: none -> 94.4 us  [local(): pl.pallas_call(kernel, out_shape=[jax.ShapeDtypeStruct(*shape) for shape...]
    all_gather x2 -> x0, waiting for transfers between devices: 91.9 us -> none  [the longest x1 64.1 us: local(): gate_full = lax.all_gather(gate_out, 'ch', axis=0, tiled=True)]
    all_to_all x2 -> x0, blocking collectives: 32.8 us -> none  [the longest x1 19.4 us: local(): lax.all_to_all(block_layout, 'seq', split_axis=1, concat_axis=2, tiled=True)]
    all_to_all x2 -> x0, starting transfers between devices: 19.3 us -> none  [the longest x1 14.2 us: local(): lax.all_to_all(monarch_product_gradient, 'seq', split_axis=2, concat_axis...]
    dot_general x12 -> x0, matrix products: 14.8 us -> none  [the longest x1 2 us: local(): lax.dot_general(w_out, hidden, (((0,), (0,)), ((), ())), preferred_elemen...]
    unnamed x54 -> x18, local copies, waits for them, and re-layouts: 24.3 us -> 10.6 us
  transfers between devices with their start and end apart: 7 -> 0, of which waited for: 4 -> 0; matrix products, arithmetic and copies ran while one was open for 6% -> 0% of each run, Pallas kernels for 0% -> 0%
where the time goes in v1:
time: 106 us
  Pallas kernels  94.4 us (89%)
  local copies, waits for them, and re-layouts  10.6 us (10%)
    pallas_call x1, Pallas kernels, local(): pl.pallas_call(kernel, out_shape=[jax.ShapeDtypeStruct(*shape) for shape...  94.4 us
    unnamed x18, local copies, waits for them, and re-layouts  10.6 us

profile of v1, /device:TPU:1, one launch (start us, length us, event | category | flops | bytes accessed | tf_op | source)
XLA Modules:
  0.0 105.7 jit_solution(6171719565628471975)
XLA Ops:
  0.6 0.0 copy-start
  0.6 1.2 %copy-done = bf16[1,8,256,256]{3,2,1,0:T(8,128)(2,1)S(1)} copy-done((bf16[1,8,256,256]{3,2,1,0:T(8,128)(2,1)S(1)}, bf16[1,8,256,256]{3,2,1,0:T(8,128)(2,1)}, u32[]{:S(2)}) %copy-start) | copy-done | bytes 1048600
  1.9 0.0 copy-start.1
  1.9 1.2 %copy-done.1 = bf16[1,8,256,256]{3,2,1,0:T(8,128)(2,1)S(1)} copy-done((bf16[1,8,256,256]{3,2,1,0:T(8,128)(2,1)S(1)}, bf16[1,8,256,256]{3,2,1,0:T(8,128)(2,1)}, u32[]{:S(2)}) %copy-start.1) | copy-done | bytes 1048600
  3.1 0.0 copy-start.2
  3.1 0.9 copy-done.2
  4.0 0.0 copy-start.3
  4.0 0.9 copy-done.3
  4.9 0.0 copy-start.4
  4.9 0.9 copy-done.4
  5.8 0.0 copy-start.5
  5.8 0.9 copy-done.5
  6.7 94.4 %monarch_block.1 = (bf16[30,2048]{1,0:T(8,128)(2,1)S(1)}, bf16[30,2048]{1,0:T(8,128)(2,1)S(1)}, bf16[8,256,256]{2,1,0:T(8,128)(2,1)S(1)}, bf16[8,256,256]{2,1,0:...) custom-call(bf16[30,2048]{1,0:T(8,128)(2,1)S(1)} %copy-done.2, ...), custom_call_target="tpu_custom_call" | custom-call | tf_op jit(solution)/shard_map/monarch_block/pallas_call | solution.py:317
  101.1 0.7 copy.18
  101.8 0.7 copy.19
  102.5 1.0 copy.20
  103.4 1.0 copy.21
  104.4 0.6 copy.22
  105.0 0.6 copy.23
Async XLA Ops:
  0.6 1.2 %copy-start = (bf16[1,8,256,256]{3,2,1,0:T(8,128)(2,1)S(1)}, bf16[1,8,256,256]{3,2,1,0:T(8,128)(2,1)}, u32[]{:S(2)}) copy-start(bf16[1,8,256,256]{3,2,1,0:T(8,128)(2,1)} %param.8) | copy-start | bytes 3145732
  1.9 1.2 %copy-start.1 = (bf16[1,8,256,256]{3,2,1,0:T(8,128)(2,1)S(1)}, bf16[1,8,256,256]{3,2,1,0:T(8,128)(2,1)}, u32[]{:S(2)}) copy-start(bf16[1,8,256,256]{3,2,1,0:T(8,128)(2,1)} %param.9) | copy-start | bytes 3145732
  3.1 0.9 copy-start.2
  4.0 0.9 copy-start.3
  4.9 0.9 copy-start.4
  5.8 0.9 copy-start.5

commit v2 on v1

v2 whole, which is shorter than its diff:
```python
import jax
import jax.numpy as jnp
from jax import lax
from jax.experimental import pallas as pl
from jax.experimental.pallas import tpu as pltpu
from jax.sharding import PartitionSpec as P

NS = 32
NC = 16
GC = 30
HID = 120
VMEM_LIMIT = 60 * 1024 * 1024
F32 = jnp.float32
BF16 = jnp.bfloat16
MESH = pl.DeviceIdType.MESH

NN = (((1,), (0,)), ((), ()))
NT = (((1,), (1,)), ((), ()))
TN = (((0,), (0,)), ((), ()))

A1, A2, A3, A4 = 0, 1, 2, 3
C1, C2, G1, G2 = 4, 8, 9, 13
WZ, WC = 14, 15
U1, U2, M1, M2 = 16, 20, 21, 22
PC, PZ, PS, PA = 23, 24, 25, 26
N_SEM = 27


def dot(a, b, dims=NN):
    return lax.dot_general(a, b, dims, preferred_element_type=F32)


def one_hot(shape, test):
    rows = lax.broadcasted_iota(jnp.int32, shape, 0)
    cols = lax.broadcasted_iota(jnp.int32, shape, 1)
    return jnp.where(test(rows, cols), 1.0, 0.0).astype(BF16)


def gelu_parts(v):
    cdf = 0.5 * (1.0 + lax.erf(v * 0.7071067811865476))
    return v * cdf, cdf + v * jnp.exp(-0.5 * v * v) * 0.3989422804014327


def kernel(
    tok_h, cot_h, r_h, l_h, wi_h, wo_h,
    mixed_h, gin_h, gr_h, gl_h, gwi_h, gwo_h,
    tok_v, cot_v, r_v, l_v, wi_v, wo_v,
    tokp, cots, s1, r1, s2, r2, s3, r3, s4, r4,
    fold_src, ct, mon, go, gf, cf, ws, w12, w1t, w2t, back, hid, pg,
    su, ru, su2, ru2, sm, rm, sm2, rm2,
    sg, sx, sp, rp, sh, rh, sf, rf, gg,
    mixed_v, gin_v, gl_v, gr_v, gwi_v, gwo_v,
    in_sem, out_sem, send_sem, recv_sem,
):
    s, c = lax.axis_index("seq"), lax.axis_index("ch")
    cx, cz = c // 4, lax.rem(c, 4)
    core = lax.rem(s, 2)
    pair = s // 2
    other = s + 1 - 2 * core

    barrier = pltpu.get_barrier_semaphore()

    @pl.loop(1, NS)
    def _(o):
        pl.semaphore_signal(barrier, inc=1, device_id={"seq": lax.rem(s + o, NS), "ch": c}, device_id_type=MESH)

    @pl.loop(1, NC)
    def _(o):
        pl.semaphore_signal(barrier, inc=1, device_id={"seq": s, "ch": lax.rem(c + o, NC)}, device_id_type=MESH)

    ins = [
        pltpu.make_async_copy(src, dst, in_sem.at[n])
        for n, (src, dst) in enumerate(
            ((tok_h, tok_v), (r_h, r_v), (cot_h, cot_v), (wi_h, wi_v), (wo_h, wo_v), (l_h, l_v))
        )
    ]
    for copy in ins:
        copy.start()

    pending = []

    def send(which, src, dst, seq, ch):
        pltpu.make_async_remote_copy(
            src_ref=src, dst_ref=dst, send_sem=send_sem.at[which], recv_sem=recv_sem.at[which],
            device_id={"seq": seq, "ch": ch}, device_id_type=MESH,
        ).start()

    def over_seq(which, src_of, dst):
        @pl.loop(1, NS)
        def _(o):
            t = lax.rem(s + o, NS)
            send(which, src_of(t), dst.at[s], t, c)

        pending.append((which, dst.at[pl.ds(0, NS - 1)]))

    def along_x(which, src, dst):
        for o in (1, 2, 3):
            send(which, src, dst, s, lax.rem(cx + o, 4) * 4 + cz)

    def along_z(o):
        return lax.rem(cz + o, 4), lax.rem(cz + 4 - o, 4)

    def arrived(which, view):
        pltpu.make_async_copy(view, view, recv_sem.at[which]).wait()

    def sent(which, view):
        pltpu.make_async_copy(view, view, send_sem.at[which]).wait()

    def gather_first(z_sem, x_sem, src, dst):
        for o in (2, 1, 3):
            to, _ = along_z(o)
            send(z_sem + o, src.at[to], dst.at[c], s, 4 * cx + to)
            pending.append((z_sem + o, dst.at[0]))
        dst[c] = src[cz]
        along_x(x_sem, src.at[cz], dst.at[c])

    def gather_second(z_sem, x_sem, dst):
        for o in (1, 3, 2):
            _, frm = along_z(o)
            arrived(z_sem + o, dst.at[0])
            along_x(x_sem, dst.at[4 * cx + frm], dst.at[4 * cx + frm])
        pending.append((x_sem, dst.at[pl.ds(0, 12)]))

    eye = one_hot((256, 256), lambda a, b: a == b)
    fold_t = one_hot((32, 256), lambda a, b: a == (b & 31))
    keep = (
        (lax.broadcasted_iota(jnp.int32, (8, 256), 1) >> 5) == lax.broadcasted_iota(jnp.int32, (8, 256), 0)
    )[None]

    def spread(n):
        row = jnp.broadcast_to(fold_src[:, n : n + 1, :], (NS, 8, 256))
        return jnp.where(keep, row, 0.0).reshape(256, 256).astype(BF16)

    def flip(rows, dst):
        stacked = jnp.concatenate([row.astype(BF16) for row in rows], axis=0)
        dst[...] = dot(eye, stacked, NT).reshape(NS, 8, 256).astype(BF16)

    ins[0].wait()
    tokp[...] = jnp.zeros_like(tokp)
    for i in range(8):
        tokp[i, 0:GC, :] = tok_v[:, 256 * i : 256 * i + 256]
    ins[1].wait()
    flip([dot(tokp[i], r_v[i], NT) for i in range(8)], s1)
    r1[s] = s1[s]
    pl.semaphore_wait(barrier, NS + NC - 2)
    over_seq(A1, lambda t: s1.at[t], r1)

    ins[2].wait()
    cots[...] = jnp.zeros_like(cots)
    for q in range(4):
        cots[q, 0:GC, :] = cot_v[:, 512 * q : 512 * q + 512]
    gather_first(C1, C2, cots, cf)
    pad_cols = one_hot(
        (GC * NC, 512), lambda a, b: (a == GC * (b >> 5) + (b & 31)) & ((b & 31) < GC)
    )
    ins[3].wait()
    ins[4].wait()
    for n, rows in enumerate((dot(wi_v[...], pad_cols, TN), dot(wo_v[...], pad_cols))):
        ws[0, n] = rows[0:64].astype(BF16)
        ws[1, n] = jnp.zeros((64, 512), BF16)
        ws[1, n, 0 : HID - 64, :] = rows[64:HID].astype(BF16)
    w12[core, cz] = ws[core]
    for o in (1, 2, 3):
        to, _ = along_z(o)
        send(WZ, ws.at[core], w12.at[core, cz], s, 4 * cx + to)
    pending.append((WZ, w12.at[0, pl.ds(0, 3)]))

    ins[5].wait()
    arrived(A1, r1.at[pl.ds(0, NS - 1)])
    fold_src[...] = r1[...].astype(F32)
    for k in range(8):
        ct[k] = dot(fold_t, spread(k), NT).astype(BF16)
    flip([dot(ct[k], l_v[k], NT) for k in range(8)], s2)
    r2[s] = s2[s]
    over_seq(A2, lambda t: s2.at[t], r2)
    gather_second(C1, C2, cf)

    arrived(A2, r2.at[pl.ds(0, NS - 1)])
    fold_src[...] = r2[...].astype(F32)
    for l in range(8):
        m = dot(fold_t, spread(l), NT)
        mon[l] = m
        t = tokp[l].astype(F32)
        go[l // 2, :, 256 * (l % 2) : 256 * (l % 2) + 256] = (t + m * (t * jax.nn.sigmoid(t))).astype(BF16)
    gather_first(G1, G2, go, gf)
    arrived(WZ, w12.at[0, pl.ds(0, 3)])
    send(WC, w12.at[core], w12.at[core], other, c)
    pending.append((WC, w12.at[0]))
    gather_second(G1, G2, gf)

    arrived(WC, w12.at[0])
    eye128 = one_hot((128, 128), lambda a, b: a == b)

    def weight(h, n):
        return w12[:, h, n].reshape(128, 512)

    for h in range(4):
        for n, turned in enumerate((w1t, w2t)):
            held = weight(h, n)
            for b in range(4):
                turned[b, :, 128 * h : 128 * h + 128] = dot(
                    eye128, held[:, 128 * b : 128 * b + 128], NT
                ).astype(BF16)
    arrived(C2, cf.at[pl.ds(0, 12)])
    cot_all = cf[...].reshape(512, 512)
    for h in range(4):
        back[h] = dot(weight(h, 1), cot_all)

    arrived(G2, gf.at[pl.ds(0, 12)])
    gate_all = gf[...].reshape(512, 512)
    for h in range(4):
        value, slope = gelu_parts(dot(weight(h, 0), gate_all))
        hid[h] = value.astype(BF16)
        pg[h] = (back[h] * slope).astype(BF16)

    def partials(weights, units, dst):
        all_units = units[...].reshape(512, 512)
        for b in range(4):
            dst[b] = dot(weights[b], all_units).reshape(4, 32, 512).astype(BF16)

    def total(parts):
        value = parts[0].astype(F32)
        for part in parts[1:]:
            value = value + part.astype(F32)
        return value

    partials(w1t, pg, su)
    for o in (2, 1, 3, 0):
        to, _ = along_z(o)
        for d in (1, 2, 3):
            x = lax.rem(cx + d, 4)
            send(U1 + o, su.at[x, to], ru.at[o, cx], s, 4 * x + cz)
        ru[o, cx] = su[cx, to]
        pending.append((U1 + o, ru.at[0, pl.ds(0, 3)]))

    for h in range(4):
        for n, (units, fed) in enumerate(((pg, gate_all), (hid, cot_all))):
            rows = dot(units[h], fed, NT).astype(BF16)
            sg[0, h, n] = rows[0:64]
            sg[1, h, n] = rows[64:128]
    send(PC, sg.at[1 - core], sx, other, c)
    pending.append((PC, sx))

    for o in (2, 1, 3, 0):
        to, _ = along_z(o)
        arrived(U1 + o, ru.at[0, pl.ds(0, 3)])
        value = total([ru[o, x] for x in range(4)]).astype(BF16)
        if o == 0:
            ru2[cz] = value
        else:
            su2[o] = value
            send(U2, su2.at[o], ru2.at[cz], s, 4 * cx + to)
    pending.append((U2, ru2.at[pl.ds(0, 3)]))

    arrived(PC, sx)
    sp[...] = (sg[core].astype(F32) + sx[...].astype(F32)).astype(BF16)
    rp[cz] = sp[cz]
    for o in (2, 1, 3):
        to, _ = along_z(o)
        send(PZ, sp.at[to], rp.at[cz], s, 4 * cx + to)
    pending.append((PZ, rp.at[pl.ds(0, 3)]))

    partials(w2t, hid, sm)
    for d in (1, 2, 3):
        x = lax.rem(cx + d, 4)
        send(M1, sm.at[x], rm.at[cx], s, 4 * x + cz)
    rm[cx] = sm[cx]
    pending.append((M1, rm.at[pl.ds(0, 3)]))

    arrived(U2, ru2.at[pl.ds(0, 3)])
    rows = []
    for l in range(8):
        at = slice(256 * (l % 2), 256 * (l % 2) + 256)
        t = tokp[l].astype(F32)
        g = cots[l // 2, :, at].astype(F32) + ru2[l // 2, :, at].astype(F32)
        gg[l] = g
        rows.append(g * (t * jax.nn.sigmoid(t)))
    flip(rows, s3)
    r3[s] = s3[s]
    over_seq(A3, lambda t: s3.at[t], r3)

    arrived(M1, rm.at[pl.ds(0, 3)])
    sm2[...] = total([rm[x] for x in range(4)]).astype(BF16)
    rm2[cz] = sm2[cz]
    for o in (2, 1, 3):
        to, _ = along_z(o)
        send(M2, sm2.at[to], rm2.at[cz], s, 4 * cx + to)
    pending.append((M2, rm2.at[pl.ds(0, 3)]))

    arrived(PZ, rp.at[pl.ds(0, 3)])
    sh[...] = total([rp[z] for z in range(4)]).reshape(16, 8, 512).astype(BF16)
    rh[pair] = sh[pair]

    @pl.loop(1, 16)
    def _(o):
        t = lax.rem(pair + o, 16)
        send(PS, sh.at[t], rh.at[pair], 2 * t + core, c)

    pending.append((PS, rh.at[pl.ds(0, 15)]))

    arrived(A3, r3.at[pl.ds(0, NS - 1)])
    fold_src[...] = r3[...].astype(F32)
    flip([dot(dot(fold_t, spread(k), NT).astype(BF16), l_v[k]) for k in range(8)], s4)
    r4[s] = s4[s]
    over_seq(A4, lambda t: s4.at[t], r4)

    arrived(PS, rh.at[pl.ds(0, 15)])
    sf[...] = jnp.sum(rh[...].astype(F32), axis=0).astype(BF16)
    rf[s] = sf[...]
    over_seq(PA, lambda t: sf, rf)

    for k in range(8):
        g = dot(spread(k), fold_t, NT).astype(BF16)
        gl_v[k] = dot(g, ct[k]).astype(BF16)

    arrived(M2, rm2.at[pl.ds(0, 3)])
    for l in range(8):
        at = slice(256 * (l % 2), 256 * (l % 2) + 256)
        value = (go[l // 2, :, at].astype(F32) + rm2[l // 2, :, at].astype(F32)).astype(BF16)
        mixed_v[:, 256 * l : 256 * l + 256] = value[0:GC]
    outs = [pltpu.make_async_copy(gl_v, gl_h, out_sem.at[0]), pltpu.make_async_copy(mixed_v, mixed_h, out_sem.at[1])]
    for copy in outs:
        copy.start()

    arrived(A4, r4.at[pl.ds(0, NS - 1)])
    fold_src[...] = r4[...].astype(F32)
    for i in range(8):
        x = spread(i)
        g = dot(x, fold_t, NT).astype(BF16)
        g_t = dot(fold_t, x, NT).astype(BF16)
        gr_v[i] = dot(g, tokp[i]).astype(BF16)
        t = tokp[i].astype(F32)
        sigma = jax.nn.sigmoid(t)
        through = gg[i] * (1.0 + mon[i] * (sigma * (1.0 + t * (1.0 - sigma))))
        value = (through + dot(g_t, r_v[i])).astype(BF16)
        gin_v[:, 256 * i : 256 * i + 256] = value[0:GC]
    outs += [pltpu.make_async_copy(gr_v, gr_h, out_sem.at[2]), pltpu.make_async_copy(gin_v, gin_h, out_sem.at[3])]
    for copy in outs[2:]:
        copy.start()

    arrived(PA, rf.at[pl.ds(0, NS - 1)])
    halves = rf[...].reshape(16, 2, 8, 512)
    g_in = jnp.concatenate([halves[0:8, k].reshape(64, 512) for k in range(2)], axis=0)
    g_out = jnp.concatenate([halves[8:16, k].reshape(64, 512) for k in range(2)], axis=0)
    gwi_v[...] = dot(pad_cols, g_in, NT)[:, 0:HID].astype(BF16)
    gwo_v[...] = dot(g_out, pad_cols, NT)[0:HID].astype(BF16)
    outs += [pltpu.make_async_copy(gwi_v, gwi_h, out_sem.at[4]), pltpu.make_async_copy(gwo_v, gwo_h, out_sem.at[5])]
    for copy in outs[4:]:
        copy.start()

    for which, view in pending:
        sent(which, view)
    for copy in outs:
        copy.wait()


def hand_over(*refs):
    held, into, out = refs[12:18], refs[18], refs[19]
    reads = [pltpu.make_async_copy(refs[m], held[m], into.at[m]) for m in range(6)]
    writes = [pltpu.make_async_copy(held[m], refs[6 + m], out.at[m]) for m in range(6)]
    for copy in reads:
        copy.start()
    for read, write in zip(reads, writes):
        read.wait()
        write.start()
    for copy in writes:
        copy.wait()


def local(tokens, cotangent, right_blocks, left_blocks, w_in, w_out):
    piece = (NS, 8, 256)
    scratch = [
        ((GC, 2048), BF16), ((GC, 2048), BF16), ((8, 256, 256), BF16), ((8, 256, 256), BF16),
        ((480, HID), BF16), ((HID, 480), BF16),
        ((8, 32, 256), BF16), ((4, 32, 512), BF16),
        (piece, BF16), (piece, BF16), (piece, BF16), (piece, BF16),
        (piece, BF16), (piece, BF16), (piece, BF16), (piece, BF16),
        (piece, F32), ((8, 32, 256), BF16), ((8, 32, 256), F32),
        ((4, 32, 512), BF16), ((16, 32, 512), BF16), ((16, 32, 512), BF16),
        ((2, 2, 64, 512), BF16), ((2, 4, 2, 64, 512), BF16),
        ((4, 128, 512), BF16), ((4, 128, 512), BF16), ((4, 128, 512), F32),
        ((4, 128, 512), BF16), ((4, 128, 512), BF16),
        ((4, 4, 32, 512), BF16), ((4, 4, 32, 512), BF16), ((4, 32, 512), BF16), ((4, 32, 512), BF16),
        ((4, 4, 32, 512), BF16), ((4, 4, 32, 512), BF16), ((4, 32, 512), BF16), ((4, 32, 512), BF16),
        ((2, 4, 2, 64, 512), BF16), ((4, 2, 64, 512), BF16), ((4, 2, 64, 512), BF16), ((4, 2, 64, 512), BF16),
        ((16, 8, 512), BF16), ((16, 8, 512), BF16), ((8, 512), BF16), ((NS, 8, 512), BF16),
        ((8, 32, 256), F32),
        ((GC, 2048), BF16), ((GC, 2048), BF16), ((8, 256, 256), BF16), ((8, 256, 256), BF16),
        ((480, HID), BF16), ((HID, 480), BF16),
    ]
    shapes = [
        ((GC, 2048), BF16), ((GC, 2048), BF16), ((8, 256, 256), BF16), ((8, 256, 256), BF16),
        ((480, HID), BF16), ((HID, 480), BF16),
    ]
    results = pl.pallas_call(
        kernel,
        out_shape=[jax.ShapeDtypeStruct(*shape) for shape in shapes],
        in_specs=[pl.BlockSpec(memory_space=pl.ANY)] * 6,
        out_specs=[pl.BlockSpec(memory_space=pl.ANY)] * 6,
        scratch_shapes=[pltpu.VMEM(*shape) for shape in scratch]
        + [pltpu.SemaphoreType.DMA((6,)), pltpu.SemaphoreType.DMA((6,))]
        + [pltpu.SemaphoreType.DMA((N_SEM,)), pltpu.SemaphoreType.DMA((N_SEM,))],
        compiler_params=pltpu.CompilerParams(
            collective_id=0, has_side_effects=True, vmem_limit_bytes=VMEM_LIMIT
        ),
        name="monarch_block",
    )(tokens, cotangent, right_blocks[0], left_blocks[0], w_in, w_out)
    mixed, gin, gr, gl, gwi, gwo = pl.pallas_call(
        hand_over,
        out_shape=[jax.ShapeDtypeStruct(*shape) for shape in shapes],
        in_specs=[pl.BlockSpec(memory_space=pl.ANY)] * 6,
        out_specs=[pl.BlockSpec(memory_space=pl.ANY)] * 6,
        scratch_shapes=[pltpu.VMEM(*shape) for shape in shapes] + [pltpu.SemaphoreType.DMA((6,))] * 2,
        compiler_params=pltpu.CompilerParams(vmem_limit_bytes=VMEM_LIMIT),
        name="hand_over",
    )(*results)
    return mixed, gin, gr[None], gl[None], gwi, gwo


def solution(mesh):
    placed = (
        P("ch", "seq"),
        P("ch", "seq"),
        P("ch", "seq", None, None),
        P("ch", "seq", None, None),
        P(None, "ch"),
        P("ch", None),
    )
    return jax.shard_map(
        local,
        mesh=mesh,
        in_specs=placed,
        out_specs=placed,
        check_vma=False,
    )
```

time: 106 us -> 90.8 us (0.86)
  local copies, waits for them, and re-layouts: 10.6 us -> 0 us
  Pallas kernels: 94.4 us -> 90 us
    unnamed x18 -> x0, local copies, waits for them, and re-layouts: 10.6 us -> none
    pallas_call x1, Pallas kernels: 94.4 us -> 87.2 us  [local(): pl.pallas_call(kernel, out_shape=[jax.ShapeDtypeStruct(*shape) for shape...]
    pallas_call x0 -> x1, Pallas kernels: none -> 2.85 us  [local(): pl.pallas_call(hand_over, out_shape=[jax.ShapeDtypeStruct(*shape) for sha...]
where the time goes in v2:
time: 90.8 us; the launch traced here: 90.6 us
  Pallas kernels  90 us (99%)
    pallas_call x1, Pallas kernels, local(): pl.pallas_call(kernel, out_shape=[jax.ShapeDtypeStruct(*shape) for shape...  87.2 us
    pallas_call x1, Pallas kernels, local(): pl.pallas_call(hand_over, out_shape=[jax.ShapeDtypeStruct(*shape) for sha...  2.85 us

profile of v2, /device:TPU:1, one launch (start us, length us, event | category | flops | bytes accessed | tf_op | source)
XLA Modules:
  0.0 90.6 jit_solution(12330208141339911599)
XLA Ops:
  0.6 87.2 %monarch_block.1 = (bf16[30,2048]{1,0:T(8,128)(2,1)}, bf16[30,2048]{1,0:T(8,128)(2,1)}, bf16[8,256,256]{2,1,0:T(8,128)(2,1)}, bf16[8,256,256]{2,1,0:T(8,128)(2,1...) custom-call(bf16[30,2048]{1,0:T(8,128)(2,1)} %tok_h.1, bf16[30,2048]{1,0:T(8,128)(2,1)} %cot_h.1, ...), custom_call_target="tpu_custom_call" | custom-call | tf_op jit(solution)/shard_map/monarch_block/pallas_call | solution.py:395
  87.8 2.9 %hand_over.1 = (bf16[30,2048]{1,0:T(8,128)(2,1)}, bf16[30,2048]{1,0:T(8,128)(2,1)}, bf16[8,256,256]{2,1,0:T(8,128)(2,1)}, bf16[8,256,256]{2,1,0:T(8,128)(2,1)}, ...) custom-call(bf16[30,2048]{1,0:T(8,128)(2,1)} %get-tuple-element.18.refs_0_, ...), custom_call_target="tpu_custom_call" | custom-call | tf_op jit(solution)/shard_map/hand_over/pallas_call | solution.py:408

commit v3 on v2

--- a/solution.py
+++ b/solution.py
@@ -22,8 +22,8 @@
 C1, C2, G1, G2 = 4, 8, 9, 13
 WZ, WC = 14, 15
 U1, U2, M1, M2 = 16, 20, 21, 22
-PC, PZ, PS, PA = 23, 24, 25, 26
-N_SEM = 27
+PC, PS, PZ, PA = 23, 27, 28, 29
+N_SEM = 30
 
 
 def dot(a, b, dims=NN):
@@ -48,7 +48,7 @@
     tokp, cots, s1, r1, s2, r2, s3, r3, s4, r4,
     fold_src, ct, mon, go, gf, cf, ws, w12, w1t, w2t, back, hid, pg,
     su, ru, su2, ru2, sm, rm, sm2, rm2,
-    sg, sx, sp, rp, sh, rh, sf, rf, gg,
+    sg, sx, sp, rp, sq, rq, sf, rf, gg,
     mixed_v, gin_v, gl_v, gr_v, gwi_v, gwo_v,
     in_sem, out_sem, send_sem, recv_sem,
 ):
@@ -233,13 +233,28 @@
         ru[o, cx] = su[cx, to]
         pending.append((U1 + o, ru.at[0, pl.ds(0, 3)]))
 
-    for h in range(4):
+    for o in (2, 1, 3, 0):
+        to, _ = along_z(o)
         for n, (units, fed) in enumerate(((pg, gate_all), (hid, cot_all))):
-            rows = dot(units[h], fed, NT).astype(BF16)
-            sg[0, h, n] = rows[0:64]
-            sg[1, h, n] = rows[64:128]
-    send(PC, sg.at[1 - core], sx, other, c)
-    pending.append((PC, sx))
+            rows = dot(units[to], fed, NT).reshape(16, 8, 512).astype(BF16)
+            sg[0, to, 8 * n : 8 * n + 8] = rows[0:8]
+            sg[1, to, 8 * n : 8 * n + 8] = rows[8:16]
+        send(PC + o, sg.at[1 - core, to], sx.at[to], other, c)
+        pending.append((PC + o, sx.at[0]))
+
+    for o in (2, 1, 3, 0):
+        to, _ = along_z(o)
+        arrived(PC + o, sx.at[0])
+        sp[to] = (sg[core, to].astype(F32) + sx[to].astype(F32)).astype(BF16)
+
+        @pl.loop(1, 16)
+        def _(n):
+            t = lax.rem(pair + n, 16)
+            send(PS, sp.at[to, t], rp.at[pair, to], 2 * t + core, c)
+
+    for z in range(4):
+        rp[pair, z] = sp[z, pair]
+    pending.append((PS, rp.at[pl.ds(0, 15)]))
 
     for o in (2, 1, 3, 0):
         to, _ = along_z(o)
@@ -251,14 +266,6 @@
             su2[o] = value
             send(U2, su2.at[o], ru2.at[cz], s, 4 * cx + to)
     pending.append((U2, ru2.at[pl.ds(0, 3)]))
-
-    arrived(PC, sx)
-    sp[...] = (sg[core].astype(F32) + sx[...].astype(F32)).astype(BF16)
-    rp[cz] = sp[cz]
-    for o in (2, 1, 3):
-        to, _ = along_z(o)
-        send(PZ, sp.at[to], rp.at[cz], s, 4 * cx + to)
-    pending.append((PZ, rp.at[pl.ds(0, 3)]))
 
     partials(w2t, hid, sm)
     for d in (1, 2, 3):
@@ -287,16 +294,13 @@
         send(M2, sm2.at[to], rm2.at[cz], s, 4 * cx + to)
     pending.append((M2, rm2.at[pl.ds(0, 3)]))
 
-    arrived(PZ, rp.at[pl.ds(0, 3)])
-    sh[...] = total([rp[z] for z in range(4)]).reshape(16, 8, 512).astype(BF16)
-    rh[pair] = sh[pair]
-
-    @pl.loop(1, 16)
-    def _(o):
-        t = lax.rem(pair + o, 16)
-        send(PS, sh.at[t], rh.at[pair], 2 * t + core, c)
-
-    pending.append((PS, rh.at[pl.ds(0, 15)]))
+    arrived(PS, rp.at[pl.ds(0, 15)])
+    sq[...] = jnp.sum(rp[...].astype(F32), axis=0).astype(BF16)
+    rq[cz] = sq[cz]
+    for o in (2, 1, 3):
+        to, _ = along_z(o)
+        send(PZ, sq.at[to], rq.at[cz], s, 4 * cx + to)
+    pending.append((PZ, rq.at[pl.ds(0, 3)]))
 
     arrived(A3, r3.at[pl.ds(0, NS - 1)])
     fold_src[...] = r3[...].astype(F32)
@@ -304,8 +308,8 @@
     r4[s] = s4[s]
     over_seq(A4, lambda t: s4.at[t], r4)
 
-    arrived(PS, rh.at[pl.ds(0, 15)])
-    sf[...] = jnp.sum(rh[...].astype(F32), axis=0).astype(BF16)
+    arrived(PZ, rq.at[pl.ds(0, 3)])
+    sf[...] = total([rq[z] for z in range(4)]).astype(BF16)
     rf[s] = sf[...]
     over_seq(PA, lambda t: sf, rf)
 
@@ -382,8 +386,8 @@
         ((4, 128, 512), BF16), ((4, 128, 512), BF16),
         ((4, 4, 32, 512), BF16), ((4, 4, 32, 512), BF16), ((4, 32, 512), BF16), ((4, 32, 512), BF16),
         ((4, 4, 32, 512), BF16), ((4, 4, 32, 512), BF16), ((4, 32, 512), BF16), ((4, 32, 512), BF16),
-        ((2, 4, 2, 64, 512), BF16), ((4, 2, 64, 512), BF16), ((4, 2, 64, 512), BF16), ((4, 2, 64, 512), BF16),
-        ((16, 8, 512), BF16), ((16, 8, 512), BF16), ((8, 512), BF16), ((NS, 8, 512), BF16),
+        ((2, 4, 16, 8, 512), BF16), ((4, 16, 8, 512), BF16), ((4, 16, 8, 512), BF16), ((16, 4, 8, 512), BF16),
+        ((4, 8, 512), BF16), ((4, 8, 512), BF16), ((8, 512), BF16), ((NS, 8, 512), BF16),
         ((8, 32, 256), F32),
         ((GC, 2048), BF16), ((GC, 2048), BF16), ((8, 256, 256), BF16), ((8, 256, 256), BF16),
         ((480, HID), BF16), ((HID, 480), BF16),

time: 90.8 us -> 86.6 us (0.954)
  Pallas kernels: 90 us -> 85.8 us
    pallas_call x1, Pallas kernels: 87.2 us -> 83 us  [local(): pl.pallas_call(kernel, out_shape=[jax.ShapeDtypeStruct(*shape) for shape...]
where the time goes in v3:
time: 86.6 us; the launch traced here: 86.4 us
  Pallas kernels  85.8 us (99%)
    pallas_call x1, Pallas kernels, local(): pl.pallas_call(kernel, out_shape=[jax.ShapeDtypeStruct(*shape) for shape...  83 us
    pallas_call x1, Pallas kernels, local(): pl.pallas_call(hand_over, out_shape=[jax.ShapeDtypeStruct(*shape) for sha...  2.85 us

profile of v3, /device:TPU:1, one launch (start us, length us, event | category | flops | bytes accessed | tf_op | source)
XLA Modules:
  0.0 86.4 jit_solution(5016601495841669276)
XLA Ops:
  0.6 83.0 %monarch_block.1 = (bf16[30,2048]{1,0:T(8,128)(2,1)}, bf16[30,2048]{1,0:T(8,128)(2,1)}, bf16[8,256,256]{2,1,0:T(8,128)(2,1)}, bf16[8,256,256]{2,1,0:T(8,128)(2,1...) custom-call(bf16[30,2048]{1,0:T(8,128)(2,1)} %tok_h.1, bf16[30,2048]{1,0:T(8,128)(2,1)} %cot_h.1, ...), custom_call_target="tpu_custom_call" | custom-call | tf_op jit(solution)/shard_map/monarch_block/pallas_call | solution.py:399
  83.6 2.9 %hand_over.1 = (bf16[30,2048]{1,0:T(8,128)(2,1)}, bf16[30,2048]{1,0:T(8,128)(2,1)}, bf16[8,256,256]{2,1,0:T(8,128)(2,1)}, bf16[8,256,256]{2,1,0:T(8,128)(2,1)}, ...) custom-call(bf16[30,2048]{1,0:T(8,128)(2,1)} %get-tuple-element.18.refs_0_, ...), custom_call_target="tpu_custom_call" | custom-call | tf_op jit(solution)/shard_map/hand_over/pallas_call | solution.py:412

commit v4 on v3

--- a/solution.py
+++ b/solution.py
@@ -224,15 +224,6 @@
             value = value + part.astype(F32)
         return value
 
-    partials(w1t, pg, su)
-    for o in (2, 1, 3, 0):
-        to, _ = along_z(o)
-        for d in (1, 2, 3):
-            x = lax.rem(cx + d, 4)
-            send(U1 + o, su.at[x, to], ru.at[o, cx], s, 4 * x + cz)
-        ru[o, cx] = su[cx, to]
-        pending.append((U1 + o, ru.at[0, pl.ds(0, 3)]))
-
     for o in (2, 1, 3, 0):
         to, _ = along_z(o)
         for n, (units, fed) in enumerate(((pg, gate_all), (hid, cot_all))):
@@ -241,6 +232,15 @@
             sg[1, to, 8 * n : 8 * n + 8] = rows[8:16]
         send(PC + o, sg.at[1 - core, to], sx.at[to], other, c)
         pending.append((PC + o, sx.at[0]))
+
+    partials(w1t, pg, su)
+    for o in (2, 1, 3, 0):
+        to, _ = along_z(o)
+        for d in (1, 2, 3):
+            x = lax.rem(cx + d, 4)
+            send(U1 + o, su.at[x, to], ru.at[o, cx], s, 4 * x + cz)
+        ru[o, cx] = su[cx, to]
+        pending.append((U1 + o, ru.at[0, pl.ds(0, 3)]))
 
     for o in (2, 1, 3, 0):
         to, _ = along_z(o)

time: 86.6 us -> 86 us (level)
  no operation moved by 1% of the time
where the time goes in v4:
time: 86 us; the launch traced here: 85.8 us
  Pallas kernels  85.2 us (99%)
    pallas_call x1, Pallas kernels, local(): pl.pallas_call(kernel, out_shape=[jax.ShapeDtypeStruct(*shape) for shape...  82.3 us
    pallas_call x1, Pallas kernels, local(): pl.pallas_call(hand_over, out_shape=[jax.ShapeDtypeStruct(*shape) for sha...  2.85 us

profile of v4, /device:TPU:1, one launch (start us, length us, event | category | flops | bytes accessed | tf_op | source)
XLA Modules:
  0.0 85.8 jit_solution(7262633997067232966)
XLA Ops:
  0.6 82.3 %monarch_block.1 = (bf16[30,2048]{1,0:T(8,128)(2,1)}, bf16[30,2048]{1,0:T(8,128)(2,1)}, bf16[8,256,256]{2,1,0:T(8,128)(2,1)}, bf16[8,256,256]{2,1,0:T(8,128)(2,1...) custom-call(bf16[30,2048]{1,0:T(8,128)(2,1)} %tok_h.1, bf16[30,2048]{1,0:T(8,128)(2,1)} %cot_h.1, ...), custom_call_target="tpu_custom_call" | custom-call | tf_op jit(solution)/shard_map/monarch_block/pallas_call | solution.py:399
  83.0 2.9 %hand_over.1 = (bf16[30,2048]{1,0:T(8,128)(2,1)}, bf16[30,2048]{1,0:T(8,128)(2,1)}, bf16[8,256,256]{2,1,0:T(8,128)(2,1)}, bf16[8,256,256]{2,1,0:T(8,128)(2,1)}, ...) custom-call(bf16[30,2048]{1,0:T(8,128)(2,1)} %get-tuple-element.18.refs_0_, ...), custom_call_target="tpu_custom_call" | custom-call | tf_op jit(solution)/shard_map/hand_over/pallas_call | solution.py:412

commit v5 on v4

--- a/solution.py
+++ b/solution.py
@@ -360,8 +360,14 @@
 
 def hand_over(*refs):
     held, into, out = refs[12:18], refs[18], refs[19]
-    reads = [pltpu.make_async_copy(refs[m], held[m], into.at[m]) for m in range(6)]
-    writes = [pltpu.make_async_copy(held[m], refs[6 + m], out.at[m]) for m in range(6)]
+    parts = [(m, slice(None)) for m in (0, 1, 4, 5)]
+    parts = [(m, pl.ds(2 * n, 2)) for n in range(4) for m in (2, 3)] + parts
+    reads = [
+        pltpu.make_async_copy(refs[m].at[at], held[m].at[at], into.at[n]) for n, (m, at) in enumerate(parts)
+    ]
+    writes = [
+        pltpu.make_async_copy(held[m].at[at], refs[6 + m].at[at], out.at[n]) for n, (m, at) in enumerate(parts)
+    ]
     for copy in reads:
         copy.start()
     for read, write in zip(reads, writes):
@@ -414,7 +420,7 @@
         out_shape=[jax.ShapeDtypeStruct(*shape) for shape in shapes],
         in_specs=[pl.BlockSpec(memory_space=pl.ANY)] * 6,
         out_specs=[pl.BlockSpec(memory_space=pl.ANY)] * 6,
-        scratch_shapes=[pltpu.VMEM(*shape) for shape in shapes] + [pltpu.SemaphoreType.DMA((6,))] * 2,
+        scratch_shapes=[pltpu.VMEM(*shape) for shape in shapes] + [pltpu.SemaphoreType.DMA((12,))] * 2,
         compiler_params=pltpu.CompilerParams(vmem_limit_bytes=VMEM_LIMIT),
         name="hand_over",
     )(*results)

time: 86 us -> 85.8 us (level)
  no operation moved by 1% of the time
where the time goes in v5:
time: 85.8 us; the launch traced here: 85.6 us
  Pallas kernels  85 us (99%)
    pallas_call x1, Pallas kernels, local(): pl.pallas_call(kernel, out_shape=[jax.ShapeDtypeStruct(*shape) for shape...  82.3 us
    pallas_call x1, Pallas kernels, local(): pl.pallas_call(hand_over, out_shape=[jax.ShapeDtypeStruct(*shape) for sha...  2.63 us

profile of v5, /device:TPU:1, one launch (start us, length us, event | category | flops | bytes accessed | tf_op | source)
XLA Modules:
  0.0 85.6 jit_solution(479161231535332290)
XLA Ops:
  0.6 82.3 %monarch_block.1 = (bf16[30,2048]{1,0:T(8,128)(2,1)}, bf16[30,2048]{1,0:T(8,128)(2,1)}, bf16[8,256,256]{2,1,0:T(8,128)(2,1)}, bf16[8,256,256]{2,1,0:T(8,128)(2,1...) custom-call(bf16[30,2048]{1,0:T(8,128)(2,1)} %tok_h.1, bf16[30,2048]{1,0:T(8,128)(2,1)} %cot_h.1, ...), custom_call_target="tpu_custom_call" | custom-call | tf_op jit(solution)/shard_map/monarch_block/pallas_call | solution.py:405
  83.0 2.6 %hand_over.1 = (bf16[30,2048]{1,0:T(8,128)(2,1)}, bf16[30,2048]{1,0:T(8,128)(2,1)}, bf16[8,256,256]{2,1,0:T(8,128)(2,1)}, bf16[8,256,256]{2,1,0:T(8,128)(2,1)}, ...) custom-call(bf16[30,2048]{1,0:T(8,128)(2,1)} %get-tuple-element.18.refs_0_, ...), custom_call_target="tpu_custom_call" | custom-call | tf_op jit(solution)/shard_map/hand_over/pallas_call | solution.py:418
